TPU v7x, 512 devices: a whole 4x8x8 slice. The times are simulated.
512 devices in a mesh: row: 16 (over x, y_lo), col: 16 (over z, core), dp: 2 (over y_hi).
Axes of the slice: x: 4, y: 8 (y_hi: 2, y_lo: 4; y = y_hi * 4 + y_lo), z: 8, core: 2. Of those that a mesh axis runs over, the one named last changes fastest.
Arguments:
- grad_output: bfloat16 [2, 2048, 8192], P('dp', 'col', 'row'), may hold values from -0.09375 to 0.09375
- block_input: bfloat16 [2, 2048, 8192], P('dp', 'col', 'row'), may hold values from -6 to 6
- query_branch: bfloat16 [2, 2048, 8192], P('dp', 'row', 'col'), may hold values from -6 to 6
- key_branch: bfloat16 [2, 2048, 8192], P('dp', 'row', 'col'), may hold values from -6 to 6
- value_branch: bfloat16 [2, 2048, 8192], P('dp', 'row', 'col'), may hold values from -6 to 6
- out_weight: bfloat16 [8192, 8192], P('row', 'col'), may hold values from -0.0625 to 0.0625
- filters: float32 [512, 128], P('col'), may hold values from -0.5 to 0.5
Outputs:
- out_weight_grad: float32 [8192, 8192], P('row', 'col')
- value_weight_grad: float32 [8192, 8192], P('col', 'row')
- filter_grad: float32 [512, 128], P('col')
All inputs are finite; a program needn't handle non-finite values.
Results may differ from a plain program's by a relative error of at most 0.0029.
Values may be sent and summed in bfloat16 or wider, within the bound.
A program may use at most 128 MiB of HBM per device.

v0:
```python
import jax
import jax.numpy as jnp
from jax import lax
from jax.sharding import PartitionSpec as P

highest = lax.Precision.HIGHEST


def toeplitz(taps, tok_rows, causal):
    filter_len = taps.shape[1]
    out_pos = lax.broadcasted_iota(jnp.int32, (tok_rows, tok_rows + filter_len), 0)
    in_pos = lax.broadcasted_iota(jnp.int32, (tok_rows, tok_rows + filter_len), 1)
    lagged = out_pos + filter_len - in_pos if causal else in_pos - out_pos
    inside = (lagged >= 0) & (lagged < filter_len)
    picked = jnp.take(taps, jnp.clip(lagged, 0, filter_len - 1), axis=1)
    return jnp.where(inside[None], picked, 0.0)


def grouped_apply(table, signal, groups):
    blocks, extent, channels = signal.shape
    split = signal.reshape(blocks, extent, groups, channels // groups)
    result = jnp.einsum("gts,bsgc->btgc", table, split, precision=highest)
    return result.reshape(blocks, table.shape[1], channels)


def taps_partial(delta_mix, mixed_ext, groups, filter_len):
    blocks, tok_rows, channels = delta_mix.shape
    left_side = delta_mix.reshape(blocks, tok_rows, groups, channels // groups)
    right_side = mixed_ext.reshape(blocks, tok_rows + filter_len, groups, channels // groups)
    products = jnp.einsum("btgc,bsgc->gts", left_side, right_side, precision=highest)
    extent = tok_rows + filter_len
    flipped = products[:, :, ::-1]
    padded = jnp.pad(flipped, ((0, 0), (0, 0), (0, tok_rows)))
    flat_rows = padded.reshape(groups, -1)[:, : tok_rows * (extent + tok_rows - 1)]
    skewed = flat_rows.reshape(groups, tok_rows, extent + tok_rows - 1)
    column_sums = jnp.sum(skewed, axis=1)
    return column_sums[:, tok_rows - 1 : tok_rows - 1 + filter_len]


def local(grad_output, block_input, query_branch, key_branch, value_branch, out_weight, filters):
    filter_len = filters.shape[1]
    groups = filters.shape[0]
    tok_rows = query_branch.shape[1]
    channels = query_branch.shape[2]
    grads_all, inputs_all = (
        lax.all_gather(grad_output[0], "col", axis=0, tiled=True),
        lax.all_gather(block_input[0], "col", axis=0, tiled=True),
    )
    row_devices = lax.axis_size("row")
    sub_width = channels // row_devices
    delta_turned = lax.psum_scatter(
        lax.dot_general(
            out_weight, grads_all, (((0,), (1,)), ((), ())), preferred_element_type=jnp.float32
        ),
        "row",
        scatter_dimension=0,
        tiled=True,
    )
    queries, keys_here, values_here = (
        lax.all_to_all(query_branch[0], "row", split_axis=1, concat_axis=0, tiled=True),
        lax.all_to_all(key_branch[0], "row", split_axis=1, concat_axis=0, tiled=True),
        lax.all_to_all(value_branch[0], "row", split_axis=1, concat_axis=0, tiled=True),
    )
    delta_out = delta_turned.T
    local_groups = sub_width // (channels // groups)
    first_group = lax.axis_index("row") * local_groups
    my_taps = lax.dynamic_slice_in_dim(filters, first_group, local_groups, 0)
    mixed = keys_here.astype(jnp.float32) * values_here.astype(jnp.float32)
    mixed_blocks = mixed.reshape(row_devices, tok_rows, sub_width)
    earlier = jnp.concatenate(
        [
            jnp.zeros((1, filter_len, sub_width), jnp.float32),
            mixed_blocks[:-1, tok_rows - filter_len :],
        ],
        axis=0,
    )
    mixed_ext = jnp.concatenate([earlier, mixed_blocks], axis=1)
    conv_out = grouped_apply(toeplitz(my_taps, tok_rows, True), mixed_ext, local_groups).reshape(
        -1, sub_width
    )
    gated = (queries.astype(jnp.float32) * conv_out).astype(jnp.bfloat16)
    delta_mix = delta_out * queries.astype(jnp.float32)
    delta_blocks = delta_mix.reshape(row_devices, tok_rows, sub_width)
    later_part = jnp.concatenate(
        [delta_blocks[1:, :filter_len], jnp.zeros((1, filter_len, sub_width), jnp.float32)], axis=0
    )
    delta_ext = jnp.concatenate([delta_blocks, later_part], axis=1)
    delta_conv = grouped_apply(toeplitz(my_taps, tok_rows, False), delta_ext, local_groups).reshape(
        -1, sub_width
    )
    delta_value = (delta_conv * keys_here.astype(jnp.float32)).astype(jnp.bfloat16)
    my_terms = taps_partial(delta_blocks, mixed_ext, local_groups, filter_len)
    taps_local = lax.dynamic_update_slice_in_dim(
        jnp.zeros(filters.shape, jnp.float32), my_terms, first_group, 0
    )
    gated_all, value_all = (
        lax.all_gather(gated, "row", axis=1, tiled=True),
        lax.all_gather(delta_value, "row", axis=1, tiled=True),
    )
    out_grad = lax.dot_general(
        grads_all, gated_all, (((0,), (0,)), ((), ())), preferred_element_type=jnp.float32
    )
    value_grad = lax.dot_general(
        value_all, inputs_all, (((0,), (0,)), ((), ())), preferred_element_type=jnp.float32
    )
    out_grad, value_grad = lax.psum((out_grad, value_grad), "dp")
    taps_total = lax.psum(taps_local, ("row", "dp"))
    return (out_grad, value_grad, taps_total)


def solution(mesh):
    in_specs = (
        P("dp", "col", "row"),
        P("dp", "col", "row"),
        P("dp", "row", "col"),
        P("dp", "row", "col"),
        P("dp", "row", "col"),
        P("row", "col"),
        P("col", None),
    )
    out_specs = (P("row", "col"), P("col", "row"), P("col", None))
    return jax.shard_map(local, mesh=mesh, in_specs=in_specs, out_specs=out_specs, check_vma=False)
```

profile of v0, /device:TPU:64, one launch (start us, length us, event | category | flops | bytes accessed | tf_op | source)
XLA Modules:
  0.0 689.4 jit_solution(379694975442089937)
XLA Ops:
  8.0 48.5 %all-gather.11.cloned.1.call-done = bf16[1,2048,512]{2,1,0:T(8,128)(2,1)} async-done(((bf16[1,128,512]{2,1,0:T(8,128)(2,1)}), bf16[1,2048,512]{2,1,0:T(8,128)(2,1)}) %all-gather.11.cloned.1.call-update) | async-done | bytes 2097168 | tf_op jit(solution)/shard_map/all_gather | solution.py:46
  56.5 4.8 fusion.2
  61.4 0.9 copy-done.2
  62.2 0.8 copy.40
  63.0 7.1 %all-to-all-start.2 = ((bf16[128,16,32]{0,2,1:T(8,128)(2,1)}), bf16[128,16,32]{0,2,1:T(8,128)(2,1)S(1)}, u32[]{:S(2)}, u32[]{:S(2)}) async-start(bf16[128,16,32]{0,2,1:T(8,128)(2,1)} %bitcast.4), calls=%async_computation.2 | async-start | bytes 262144 | tf_op jit(solution)/shard_map/all_to_all | solution.py:62
  71.1 0.8 copy.38
  71.9 109.0 %gather_fusion = f32[32768,2]{1,0:T(8,128)} fusion(f32[2,128]{0,1:T(8,128)S(1)} %copy.62, s32[32768]{0:T(1024)S(1)} %broadcast_clamp_fusion.1), kind=kCustom, calls=%fused_computation.clone | custom fusion | bytes 655360 | tf_op jit(solution)/shard_map/jit(_take)/gather | solution.py:15
  180.9 10.0 %copy.46 = f32[128,256,2]{1,0,2:T(8,128)S(1)} copy(f32[128,256,2]{2,1,0:T(8,128)} %bitcast.113) | data formatting | bytes 524288 | tf_op jit(solution)/shard_map/jit(_take)/gather | solution.py:15
  190.9 0.8 copy.36
  191.9 7.5 %all-to-all-start.1 = ((bf16[128,16,32]{0,2,1:T(8,128)(2,1)}), bf16[128,16,32]{0,2,1:T(8,128)(2,1)S(1)}, u32[]{:S(2)}, u32[]{:S(2)}) async-start(bf16[128,16,32]{0,2,1:T(8,128)(2,1)} %bitcast.2), calls=%async_computation.1 | async-start | bytes 262144 | tf_op jit(solution)/shard_map/all_to_all | solution.py:61
  199.4 8.4 %all-to-all-done.1 = bf16[128,16,32]{0,2,1:T(8,128)(2,1)S(1)} async-done(((bf16[128,16,32]{0,2,1:T(8,128)(2,1)}), bf16[128,16,32]{0,2,1:T(8,128)(2,1)S(1)}, u32[]{:S(2)}, u32[]{:S(2)}) %all-to-all-start.1) | async-done | bytes 131104 | tf_op jit(solution)/shard_map/all_to_all | solution.py:61
  207.8 3.5 all-to-all-start
  212.4 7.3 %all-to-all-done = bf16[128,16,32]{0,2,1:T(8,128)(2,1)S(1)} async-done(((bf16[128,16,32]{0,2,1:T(8,128)(2,1)}), bf16[128,16,32]{0,2,1:T(8,128)(2,1)S(1)}, u32[]{:S(2)}, u32[]{:S(2)}) %all-to-all-start) | async-done | bytes 131104 | tf_op jit(solution)/shard_map/all_to_all | solution.py:60
  219.6 1.7 bitcast_multiply_fusion.2
  222.2 109.0 %gather_fusion.1 = f32[32768,2]{1,0:T(8,128)} fusion(f32[2,128]{0,1:T(8,128)S(1)} %copy.62, s32[32768]{0:T(1024)S(1)} %broadcast_clamp_fusion), kind=kCustom, calls=%fused_computation.1.clone | custom fusion | bytes 655360 | tf_op jit(solution)/shard_map/jit(_take)/gather | solution.py:15
  331.2 10.1 %copy.51 = f32[128,256,2]{1,0,2:T(8,128)S(1)} copy(f32[128,256,2]{2,1,0:T(8,128)} %bitcast.112) | data formatting | bytes 524288 | tf_op jit(solution)/shard_map/jit(_take)/gather | solution.py:15
  343.2 4.5 fusion.6
  347.7 1.5 all-gather.13.cloned.1.call-done
  349.2 91.4 %all-gather.9.cloned.1.call-done = bf16[2048,512]{0,1:T(8,128)(2,1)} async-done(((bf16[2048,32]{0,1:T(8,128)(2,1)}), bf16[2048,512]{0,1:T(8,128)(2,1)}) %all-gather.9.cloned.1.call-update) | async-done | bytes 2097168 | tf_op jit(solution)/shard_map/all_gather | solution.py:98
  440.6 4.4 fusion
  445.1 0.8 convolution_bitcast_fusion
  447.4 231.5 %psum.23 = f32[32,128]{1,0:T(8,128)} all-reduce(f32[32,128]{1,0:T(8,128)S(1)} %slice_dynamic-update-slice_fusion), channel_id=1, replica_groups=mesh['row'=16,'col'=16,'dp'=2] {'row','dp'}, use_global_device_ids=true, to_apply=%region_4.6 | all-reduce | flops 4096 | bytes 32768 | tf_op jit(solution)/shard_map/psum | solution.py:107
  678.9 2.6 copy.54
  681.5 1.0 copy.88
  (63 shorter events, 7.1 us)
Async XLA Ops:
  7.2 49.3 %copy-start = (bf16[512,512]{1,0:T(8,128)(2,1)S(1)}, bf16[512,512]{1,0:T(8,128)(2,1)}, u32[]{:S(2)}) copy-start(bf16[512,512]{1,0:T(8,128)(2,1)} %param.14) | copy-start | bytes 1572868
  7.2 49.3 %all-gather.11.cloned.1.call-start = ((), (), s32[]{:S(2)}) async-start(), calls=%async_computation.7 | async-start | bytes 2228224 | tf_op jit(solution)/shard_map/all_gather | solution.py:46
  7.9 211.7 %reduce-scatter.2.cloned.1.call-start = ((), (), s32[]{:S(2)}) async-start(), calls=%async_computation.5 | async-start | bytes 4456448 | tf_op jit(solution)/shard_map/reduce_scatter | solution.py:51
  61.3 0.9 copy-start.2
  61.3 9.7 %copy-start.3 = (bf16[1,128,512]{2,1,0:T(8,128)(2,1)S(1)}, bf16[1,128,512]{2,1,0:T(8,128)(2,1)}, u32[]{:S(2)}) copy-start(bf16[1,128,512]{2,1,0:T(8,128)(2,1)} %param.12) | copy-start | bytes 393220
  63.0 128.9 %all-to-all-start.2 = ((bf16[128,16,32]{0,2,1:T(8,128)(2,1)}), bf16[128,16,32]{0,2,1:T(8,128)(2,1)S(1)}, u32[]{:S(2)}, u32[]{:S(2)}) async-start(bf16[128,16,32]{0,2,1:T(8,128)(2,1)} %bitcast.4), calls=%async_computation.2 | async-start | bytes 262144 | tf_op jit(solution)/shard_map/all_to_all | solution.py:62
  180.9 10.0 %copy-start.4 = (bf16[1,128,512]{2,1,0:T(8,128)(2,1)S(1)}, bf16[1,128,512]{2,1,0:T(8,128)(2,1)}, u32[]{:S(2)}) copy-start(bf16[1,128,512]{2,1,0:T(8,128)(2,1)} %param.11) | copy-start | bytes 393220
  191.9 15.9 %all-to-all-start.1 = ((bf16[128,16,32]{0,2,1:T(8,128)(2,1)}), bf16[128,16,32]{0,2,1:T(8,128)(2,1)S(1)}, u32[]{:S(2)}, u32[]{:S(2)}) async-start(bf16[128,16,32]{0,2,1:T(8,128)(2,1)} %bitcast.2), calls=%async_computation.1 | async-start | bytes 262144 | tf_op jit(solution)/shard_map/all_to_all | solution.py:61
  207.8 11.9 %all-to-all-start = ((bf16[128,16,32]{0,2,1:T(8,128)(2,1)}), bf16[128,16,32]{0,2,1:T(8,128)(2,1)S(1)}, u32[]{:S(2)}, u32[]{:S(2)}) async-start(bf16[128,16,32]{0,2,1:T(8,128)(2,1)} %bitcast), calls=%async_computation | async-start | bytes 262144 | tf_op jit(solution)/shard_map/all_to_all | solution.py:60
  211.3 131.9 %all-gather.7.cloned.1.call-start = ((), (), s32[]{:S(2)}) async-start(), calls=%async_computation.4 | async-start | bytes 2228224 | tf_op jit(solution)/shard_map/all_gather | solution.py:97
  221.4 127.9 %all-gather.13.cloned.1.call-start = ((), (), s32[]{:S(2)}) async-start(), calls=%async_computation.8 | async-start | bytes 2228224 | tf_op jit(solution)/shard_map/all_gather | solution.py:47
  222.0 218.7 %all-gather.9.cloned.1.call-start = ((), (), s32[]{:S(2)}) async-start(), calls=%async_computation.6 | async-start | bytes 2228224 | tf_op jit(solution)/shard_map/all_gather | solution.py:98
  343.2 335.8 %all-reduce.6.cloned.1.call-start = ((), (), s32[]{:S(2)}) async-start(), calls=%async_computation.9 | async-start | bytes 4194304 | tf_op jit(solution)/shard_map/psum | solution.py:106
  678.9 2.6 copy-start.1
Sparse Core Ops, SparseCore 0:
  10.1 46.3 all-gather.10
  61.5 105.1 reduce-scatter.1
  221.5 84.2 all-gather.6
  307.8 41.4 all-gather.12
  351.7 88.8 all-gather.8
  445.2 122.4 all-reduce.5
where the time goes:
time: 690 us; the launch traced here: 689 us
  local copies, waits for them, and re-layouts  248 us (36%)
  blocking collectives  232 us (34%)
  waiting for transfers between devices  158 us (23%)
  starting transfers between devices  18.4 us (3%)
  matrix products  15.8 us (2%)
  between operations  14.4 us (2%)
    gather x4, local copies, waits for them, and re-layouts, toeplitz(): picked = jnp.take(taps, jnp.clip(lagged, 0, filter_len - 1), axis=1)  238 us
    psum x1, blocking collectives, local(): taps_total = lax.psum(taps_local, ('row', 'dp'))  232 us
    all_gather x1, waiting for transfers between devices, local(): lax.all_gather(delta_value, 'row', axis=1, tiled=True)  91.4 us
    all_gather x1, waiting for transfers between devices, local(): lax.all_gather(grad_output[0], 'col', axis=0, tiled=True)  48.5 us
  transfers between devices with their start and end apart: 9, of which 5 were waited for; matrix products, arithmetic and copies ran while one was open for 36% of the time, Pallas kernels for 0%

commit v1 on v0

--- a/solution.py
+++ b/solution.py
@@ -1,9 +1,21 @@
+import functools
 import jax
 import jax.numpy as jnp
 from jax import lax
 from jax.sharding import PartitionSpec as P
 
 highest = lax.Precision.HIGHEST
+
+
+def touch_the_results(target, device_axis):
+    carry_out = jax.lax.psum(1, device_axis)
+    s_next = jnp.stack(carry_out * [target])
+    q_next = jax.lax.all_to_all(s_next, device_axis, 0, 0)
+    b_next = jnp.concatenate(q_next, axis=1)
+    return b_next
+
+
+_fill_links = functools.partial(touch_the_results, device_axis="row")
 
 
 def toeplitz(taps, tok_rows, causal):
@@ -95,7 +107,7 @@
     )
     gated_all, value_all = (
         lax.all_gather(gated, "row", axis=1, tiled=True),
-        lax.all_gather(delta_value, "row", axis=1, tiled=True),
+        _fill_links(delta_value),
     )
     out_grad = lax.dot_general(
         grads_all, gated_all, (((0,), (0,)), ((), ())), preferred_element_type=jnp.float32

time: 690 us -> 641 us (0.929)
  the two profiles are of different devices: /device:TPU:64 before, /device:TPU:40 now
where the time goes in v1:
time: 641 us; the launch traced here: 640 us
  local copies, waits for them, and re-layouts  248 us (39%)
  blocking collectives  234 us (37%)
  waiting for transfers between devices  103 us (16%)
  starting transfers between devices  22.7 us (4%)
  matrix products  15.2 us (2%)
  between operations  14.1 us (2%)
    gather x4, local copies, waits for them, and re-layouts, toeplitz(): picked = jnp.take(taps, jnp.clip(lagged, 0, filter_len - 1), axis=1)  237 us
    psum x1, blocking collectives, local(): taps_total = lax.psum(taps_local, ('row', 'dp'))  234 us
    all_gather x1, waiting for transfers between devices, local(): lax.all_gather(grad_output[0], 'col', axis=0, tiled=True)  49.6 us
    all_to_all x1, waiting for transfers between devices, touch_the_results(): q_next = jax.lax.all_to_all(s_next, device_axis, 0, 0)  38.9 us
  transfers between devices with their start and end apart: 9, of which 4 were waited for; matrix products, arithmetic and copies ran while one was open for 39% of the time, Pallas kernels for 0%

profile of v1, /device:TPU:40, one launch (start us, length us, event | category | flops | bytes accessed | tf_op | source)
XLA Modules:
  0.0 640.3 jit_solution(6153766318672468249)
XLA Ops:
  8.0 49.6 %all-gather.8.cloned.1.call-done = bf16[1,2048,512]{2,1,0:T(8,128)(2,1)} async-done(((bf16[1,128,512]{2,1,0:T(8,128)(2,1)}), bf16[1,2048,512]{2,1,0:T(8,128)(2,1)}) %all-gather.8.cloned.1.call-update) | async-done | bytes 2097168 | tf_op jit(solution)/shard_map/all_gather | solution.py:58
  57.6 4.8 fusion.2
  62.4 0.9 copy-done.2
  63.3 0.8 copy.40
  64.1 5.8 all-to-all-start.2
  70.8 0.8 copy.38
  71.6 108.5 %gather_fusion = f32[32768,2]{1,0:T(8,128)} fusion(f32[2,128]{0,1:T(8,128)S(1)} %copy.62, s32[32768]{0:T(1024)S(1)} %broadcast_clamp_fusion.1), kind=kCustom, calls=%fused_computation.clone | custom fusion | bytes 655360 | tf_op jit(solution)/shard_map/jit(_take)/gather | solution.py:27
  180.1 10.0 %copy.46 = f32[128,256,2]{1,0,2:T(8,128)S(1)} copy(f32[128,256,2]{2,1,0:T(8,128)} %bitcast.116) | data formatting | bytes 524288 | tf_op jit(solution)/shard_map/jit(_take)/gather | solution.py:27
  191.0 7.5 %all-to-all-start.1 = ((bf16[128,16,32]{0,2,1:T(8,128)(2,1)}), bf16[128,16,32]{0,2,1:T(8,128)(2,1)S(1)}, u32[]{:S(2)}, u32[]{:S(2)}) async-start(bf16[128,16,32]{0,2,1:T(8,128)(2,1)} %bitcast.2), calls=%async_computation.1 | async-start | bytes 262144 | tf_op jit(solution)/shard_map/all_to_all | solution.py:73
  198.6 7.3 %all-to-all-done.1 = bf16[128,16,32]{0,2,1:T(8,128)(2,1)S(1)} async-done(((bf16[128,16,32]{0,2,1:T(8,128)(2,1)}), bf16[128,16,32]{0,2,1:T(8,128)(2,1)S(1)}, u32[]{:S(2)}, u32[]{:S(2)}) %all-to-all-start.1) | async-done | bytes 131104 | tf_op jit(solution)/shard_map/all_to_all | solution.py:73
  205.8 4.5 all-to-all-start
  211.5 6.3 all-to-all-done
  217.7 1.7 bitcast_multiply_fusion.2
  220.3 108.5 %gather_fusion.1 = f32[32768,2]{1,0:T(8,128)} fusion(f32[2,128]{0,1:T(8,128)S(1)} %copy.62, s32[32768]{0:T(1024)S(1)} %broadcast_clamp_fusion), kind=kCustom, calls=%fused_computation.1.clone | custom fusion | bytes 655360 | tf_op jit(solution)/shard_map/jit(_take)/gather | solution.py:27
  328.8 10.1 %copy.51 = f32[128,256,2]{1,0,2:T(8,128)S(1)} copy(f32[128,256,2]{2,1,0:T(8,128)} %bitcast.115) | data formatting | bytes 524288 | tf_op jit(solution)/shard_map/jit(_take)/gather | solution.py:27
  340.0 1.6 stack.2
  341.6 4.7 all-to-all-start.3
  346.3 4.5 fusion.6
  350.8 38.9 %all-to-all-done.3 = bf16[16,2048,32]{1,2,0:T(8,128)(2,1)S(1)} async-done(((bf16[16,2048,32]{1,2,0:T(8,128)(2,1)}), bf16[16,2048,32]{1,2,0:T(8,128)(2,1)S(1)}, u32[]{:S(2)}, u32[]{:S(2)}) %all-to-all-start.3) | async-done | bytes 2097184 | tf_op jit(solution)/shard_map/all_to_all | solution.py:13
  389.7 3.8 fusion
  393.6 0.8 convolution_bitcast_fusion
  395.8 234.3 %psum.23 = f32[32,128]{1,0:T(8,128)} all-reduce(f32[32,128]{1,0:T(8,128)S(1)} %slice_dynamic-update-slice_fusion), channel_id=1, replica_groups=mesh['row'=16,'col'=16,'dp'=2] {'row','dp'}, use_global_device_ids=true, to_apply=%region_4.6 | all-reduce | flops 4096 | bytes 32768 | tf_op jit(solution)/shard_map/psum | solution.py:119
  630.1 2.6 copy.54
  632.8 1.0 copy.88
  (63 shorter events, 7.1 us)
Async XLA Ops:
  7.2 50.4 %copy-start = (bf16[512,512]{1,0:T(8,128)(2,1)S(1)}, bf16[512,512]{1,0:T(8,128)(2,1)}, u32[]{:S(2)}) copy-start(bf16[512,512]{1,0:T(8,128)(2,1)} %param.14) | copy-start | bytes 1572868
  7.2 50.4 %all-gather.8.cloned.1.call-start = ((), (), s32[]{:S(2)}) async-start(), calls=%async_computation.7 | async-start | bytes 2228224 | tf_op jit(solution)/shard_map/all_gather | solution.py:58
  7.9 209.8 %reduce-scatter.2.cloned.1.call-start = ((), (), s32[]{:S(2)}) async-start(), calls=%async_computation.6 | async-start | bytes 4456448 | tf_op jit(solution)/shard_map/reduce_scatter | solution.py:63
  62.4 0.9 copy-start.2
  62.4 8.4 %copy-start.3 = (bf16[1,128,512]{2,1,0:T(8,128)(2,1)S(1)}, bf16[1,128,512]{2,1,0:T(8,128)(2,1)}, u32[]{:S(2)}) copy-start(bf16[1,128,512]{2,1,0:T(8,128)(2,1)} %param.12) | copy-start | bytes 393220
  64.1 127.0 %all-to-all-start.2 = ((bf16[128,16,32]{0,2,1:T(8,128)(2,1)}), bf16[128,16,32]{0,2,1:T(8,128)(2,1)S(1)}, u32[]{:S(2)}, u32[]{:S(2)}) async-start(bf16[128,16,32]{0,2,1:T(8,128)(2,1)} %bitcast.4), calls=%async_computation.2 | async-start | bytes 262144 | tf_op jit(solution)/shard_map/all_to_all | solution.py:74
  180.1 10.0 %copy-start.4 = (bf16[1,128,512]{2,1,0:T(8,128)(2,1)S(1)}, bf16[1,128,512]{2,1,0:T(8,128)(2,1)}, u32[]{:S(2)}) copy-start(bf16[1,128,512]{2,1,0:T(8,128)(2,1)} %param.11) | copy-start | bytes 393220
  191.0 14.8 %all-to-all-start.1 = ((bf16[128,16,32]{0,2,1:T(8,128)(2,1)}), bf16[128,16,32]{0,2,1:T(8,128)(2,1)S(1)}, u32[]{:S(2)}, u32[]{:S(2)}) async-start(bf16[128,16,32]{0,2,1:T(8,128)(2,1)} %bitcast.2), calls=%async_computation.1 | async-start | bytes 262144 | tf_op jit(solution)/shard_map/all_to_all | solution.py:73
  205.8 11.9 %all-to-all-start = ((bf16[128,16,32]{0,2,1:T(8,128)(2,1)}), bf16[128,16,32]{0,2,1:T(8,128)(2,1)S(1)}, u32[]{:S(2)}, u32[]{:S(2)}) async-start(bf16[128,16,32]{0,2,1:T(8,128)(2,1)} %bitcast), calls=%async_computation | async-start | bytes 262144 | tf_op jit(solution)/shard_map/all_to_all | solution.py:72
  210.4 136.0 %all-gather.6.cloned.1.call-start = ((), (), s32[]{:S(2)}) async-start(), calls=%async_computation.5 | async-start | bytes 2228224 | tf_op jit(solution)/shard_map/all_gather | solution.py:109
  219.5 131.3 %all-gather.10.cloned.1.call-start = ((), (), s32[]{:S(2)}) async-start(), calls=%async_computation.8 | async-start | bytes 2228224 | tf_op jit(solution)/shard_map/all_gather | solution.py:59
  341.6 48.1 %all-to-all-start.3 = ((bf16[16,2048,32]{1,2,0:T(8,128)(2,1)}), bf16[16,2048,32]{1,2,0:T(8,128)(2,1)S(1)}, u32[]{:S(2)}, u32[]{:S(2)}) async-start(bf16[16,2048,32]{1,2,0:T(8,128)(2,1)} %stack.2), calls=%async_computation.4 | async-start | bytes 4194304 | tf_op jit(solution)/shard_map/all_to_all | solution.py:13
  346.3 283.9 %all-reduce.6.cloned.1.call-start = ((), (), s32[]{:S(2)}) async-start(), calls=%async_computation.9 | async-start | bytes 4194304 | tf_op jit(solution)/shard_map/psum | solution.py:118
  630.1 2.6 copy-start.1
Sparse Core Ops, SparseCore 0:
  10.1 47.3 all-gather.7
  62.5 100.3 reduce-scatter.1
  219.6 84.8 all-gather.5
  306.4 43.7 all-gather.9
  393.7 126.0 all-reduce.5
